TPU v7x, 256 devices: a whole 4x4x8 slice. The times are simulated.
256 devices in a mesh: seq: 16 (over z, core), rep: 16 (over x, y).
Axes of the slice: x: 4, y: 4, z: 8, core: 2. Of those that a mesh axis runs over, the one named last changes fastest.
Arguments:
- tokens: bfloat16 [65536, 1024], P(('rep', 'seq')), parts along dimension 0, may hold values from -16 to 16
- segments: int32 [65536], P(('rep', 'seq')), parts along dimension 0, may hold values from 0 to 3, never falling along the last dimension, each value on 1 to 2048 neighbouring positions
- qkv_weight: bfloat16 [1024, 3072], replicated, may hold values from -1 to 1
- out_weight: bfloat16 [1024, 1024], replicated, may hold values from -0.1875 to 0.1875
- out_bias: float32 [1024], replicated, may hold values from -3 to 3
- ln_gain: float32 [1024], replicated, may hold values from 0.1 to 1.9
- ln_bias: float32 [1024], replicated, may hold values from -3 to 3
Outputs:
- normed: bfloat16 [65536, 1024], P(('rep', 'seq')), parts along dimension 0
- kv_cache: bfloat16 [65536, 2048], P('rep', 'seq'), parts along dimension 0
There are 16 independent parts, one for each index of `rep`. A program takes and returns all parts, laid end to end along the dimension named above; an argument that names none is the same for every part. Nothing has to cross between parts.
Inputs may be any that keep to these rules, and one draw needn't show every extreme that they name: `segments`: each prompt is a contiguous run of 1 to 2048 tokens, numbers never falling, one prompt exactly 2048 tokens.
All inputs are finite; a program needn't handle non-finite values.
Results may differ from a plain program's by a relative error of at most 0.008.
Values may be sent and summed in bfloat16 or wider, within the bound.
A program may use at most 128 MiB of HBM per device.

v0:
```python
import math
import jax
import jax.numpy as jnp
from jax import lax
from jax.sharding import PartitionSpec as P

HEADS = 16
HEAD = 64


def shards(tokens, segments, qkv_weight, out_weight, out_bias, ln_gain, ln_bias):
    tok_rows, width = tokens.shape
    scale = 1.0 / math.sqrt(HEAD)
    all_seg = lax.all_gather(segments, "seq", axis=0, tiled=True)
    proj = jnp.dot(tokens, qkv_weight, preferred_element_type=jnp.float32).astype(jnp.bfloat16)
    grouped = proj.reshape(tok_rows, HEADS, 3, HEAD)
    key_value = grouped[:, :, 1:, :].reshape(tok_rows, 2 * width)
    kv_cache = lax.all_to_all(key_value, "seq", split_axis=1, concat_axis=0, tiled=True)
    queries = jnp.moveaxis(grouped[:, :, 0, :], 1, 0)
    piece = lax.all_gather(key_value, "seq", axis=0, tiled=True)
    top_now = jnp.full((HEADS, tok_rows), -1e30, jnp.float32)
    total_now = jnp.zeros((HEADS, tok_rows), jnp.float32)
    acc_now = jnp.zeros((HEADS, tok_rows, HEAD), jnp.float32)
    count_rows = piece.shape[0]
    kept = segments[:, None] == all_seg[None, :]
    split_piece = piece.reshape(count_rows, HEADS, 2, HEAD)
    keys = jnp.moveaxis(split_piece[:, :, 0, :], 1, 0)
    values = jnp.moveaxis(split_piece[:, :, 1, :], 1, 0)

    def per_head(items):
        query, key_h, value_h, top_h, total_h, acc_h = items
        score = jnp.dot(query, key_h.T, preferred_element_type=jnp.float32) * scale
        score = jnp.where(kept, score, -1e30)
        new_top = jnp.maximum(top_h, jnp.max(score, axis=1))
        weight = jnp.where(kept, jnp.exp(score - new_top[:, None]), 0.0)
        factor = jnp.exp(top_h - new_top)
        new_total = total_h * factor + jnp.sum(weight, axis=1)
        new_acc = acc_h * factor[:, None] + jnp.dot(
            weight.astype(jnp.bfloat16), value_h, preferred_element_type=jnp.float32
        )
        return (new_top, new_total, new_acc)

    top_all, total_all, acc_all = lax.map(
        per_head, (queries, keys, values, top_now, total_now, acc_now)
    )
    context = (acc_all / total_all[:, :, None]).astype(jnp.bfloat16)
    gathered_ctx = jnp.moveaxis(context, 0, 1).reshape(tok_rows, width)
    mixed = (
        jnp.dot(gathered_ctx, out_weight, preferred_element_type=jnp.float32)
        + out_bias
        + tokens.astype(jnp.float32)
    )
    mean = jnp.mean(mixed, axis=1, keepdims=True)
    centered = mixed - mean
    variance = jnp.mean(centered * centered, axis=1, keepdims=True)
    normed = centered / jnp.sqrt(variance + 1e-05) * ln_gain + ln_bias
    return (normed.astype(jnp.bfloat16), kv_cache)


def solution(mesh):
    in_specs = (P(("rep", "seq"), None), P(("rep", "seq")), P(), P(), P(), P(), P())
    out_specs = (P(("rep", "seq"), None), P("rep", "seq"))
    return jax.shard_map(shards, mesh=mesh, in_specs=in_specs, out_specs=out_specs, check_vma=False)
```

profile of v0, /device:TPU:1, one launch (start us, length us, event | category | flops | bytes accessed | tf_op | source)
XLA Modules:
  0.0 246.1 jit_solution(5084389880568863316)
XLA Ops:
  7.2 6.0 %convolution_convert_fusion = bf16[256,3072]{1,0:T(8,128)(2,1)} fusion(bf16[256,1024]{1,0:T(8,128)(2,1)} %param.9, bf16[1024,3072]{1,0:T(8,128)(2,1)} %param.11), kind=kOutput, calls=%fused_computation.24 | convolution fusion | flops 1611399168 | bytes 8388608 | tf_op jit(solution)/shard_map/dot_general | solution.py:15
  13.3 2.6 %copy.20 = bf16[256,3072]{0,1:T(8,128)(2,1)} copy(bf16[256,3072]{1,0:T(8,128)(2,1)} %convolution_convert_fusion) | data formatting | bytes 3145728 | tf_op jit(solution)/shard_map/convert_element_type | solution.py:15
  15.9 2.3 slice.17
  18.2 10.0 %all-to-all-start = ((bf16[256,16,128]{0,2,1:T(8,128)(2,1)}), bf16[256,16,128]{0,2,1:T(8,128)(2,1)S(1)}, u32[]{:S(2)}, u32[]{:S(2)}) async-start(bf16[256,16,128]{0,2,1:T(8,128)(2,1)} %bitcast.60), calls=%async_computation | async-start | bytes 2097152 | tf_op jit(solution)/shard_map/all_to_all | solution.py:18
  28.2 46.9 %all-gather = s32[16,1,256]{2,1,0:T(1,128)S(1)} all-gather(s32[1,1,256]{2,1,0:T(1,128)S(1)} %bitcast.68), channel_id=1, replica_groups=mesh['seq'=16,'rep'=16] {'seq'}, dimensions={0}, use_global_device_ids=true | all-gather | bytes 17408 | tf_op jit(solution)/shard_map/all_gather | solution.py:14
  78.3 64.8 %all-gather.3.cloned.1.call-done = bf16[4096,2048]{0,1:T(8,128)(2,1)} async-done(((bf16[256,2048]{0,1:T(8,128)(2,1)}), bf16[4096,2048]{0,1:T(8,128)(2,1)}) %all-gather.3.cloned.1.call-update) | async-done | bytes 16777232 | tf_op jit(solution)/shard_map/all_gather | solution.py:20
  143.1 11.8 %slice_bitcast_fusion = (bf16[16,4096,64]{1,2,0:T(8,128)(2,1)}, bf16[16,4096,64]{1,2,0:T(8,128)(2,1)}) fusion(bf16[4096,16,2,64]{0,3,2,1:T(8,128)(2,1)} %bitcast.58), kind=kLoop, calls=%fused_computation.22 | loop fusion | bytes 33554432 | tf_op jit(solution)/shard_map/transpose | solution.py:28
  154.9 81.0 %while.13 = (s32[]{:T(128)}, f32[16,256]{1,0:T(8,128)S(1)}, f32[16,256,64]{1,2,0:T(8,128)S(1)}, bf16[16,256,64]{1,2,0:T(8,128)(2,1)}, bf16[16,4096,64]{1,2,0:T(8...) while((s32[]{:T(128)}, f32[16,256]{1,0:T(8,128)S(1)}, ...), condition=%wide.region_3.4_spmd.clone, body=%wide.region_0.3_spmd.clone.sunk | while | flops 281035520 | bytes 13797481 | solution.py:43
  157.9 2.0 fusion.42
  163.0 2.0 fusion.42
  168.0 2.0 fusion.42
  173.1 2.0 fusion.42
  178.2 2.0 fusion.42
  183.2 2.0 fusion.42
  188.3 2.0 fusion.42
  193.3 2.0 fusion.42
  198.4 2.0 fusion.42
  203.5 2.0 fusion.42
  208.5 2.0 fusion.42
  213.6 2.0 fusion.42
  218.7 2.0 fusion.42
  223.7 2.0 fusion.42
  228.8 2.0 fusion.42
  233.8 2.0 fusion.42
  (105 shorter events, 54.9 us)
Async XLA Ops:
  7.2 228.9 %copy-start = (bf16[1024,1024]{1,0:T(8,128)(2,1)S(1)}, bf16[1024,1024]{1,0:T(8,128)(2,1)}, u32[]{:S(2)}) copy-start(bf16[1024,1024]{1,0:T(8,128)(2,1)} %param.12) | copy-start | bytes 6291460
  7.2 136.0 %all-gather.3.cloned.1.call-start = ((), (), s32[]{:S(2)}) async-start(), calls=%async_computation.1 | async-start | bytes 17825792 | tf_op jit(solution)/shard_map/all_gather | solution.py:20
  13.3 14.9 %copy-start.2 = (s32[256]{0:T(256)S(1)}, s32[256]{0:T(256)}, u32[]{:S(2)}) copy-start(s32[256]{0:T(256)} %param.10) | copy-start | bytes 3076
  18.2 58.8 %all-to-all-start = ((bf16[256,16,128]{0,2,1:T(8,128)(2,1)}), bf16[256,16,128]{0,2,1:T(8,128)(2,1)S(1)}, u32[]{:S(2)}, u32[]{:S(2)}) async-start(bf16[256,16,128]{0,2,1:T(8,128)(2,1)} %bitcast.60), calls=%async_computation | async-start | bytes 2097152 | tf_op jit(solution)/shard_map/all_to_all | solution.py:18
  143.1 11.8 %copy-start.1 = (f32[16,256,64]{1,2,0:T(8,128)S(1)}, f32[16,256,64]{1,2,0:T(8,128)}, u32[]{:S(2)}) copy-start(f32[16,256,64]{1,2,0:T(8,128)} %custom-call.1) | copy-start | bytes 3145732
  154.9 81.1 %copy-start.3 = (f32[1024]{0:T(1024)S(1)}, f32[1024]{0:T(1024)}, u32[]{:S(2)}) copy-start(f32[1024]{0:T(1024)} %param.13) | copy-start | bytes 12292
  235.9 2.3 copy-start.4
  235.9 2.3 copy-start.5
Sparse Core Ops, SparseCore 0:
  18.3 124.7 all-gather.2
where the time goes:
time: 248 us; the launch traced here: 246 us
  matrix products  71.4 us (29%)
  waiting for transfers between devices  64.8 us (26%)
  blocking collectives  46.9 us (19%)
  local copies, waits for them, and re-layouts  20.6 us (8%)
  other arithmetic  17.7 us (7%)
  between operations  14.1 us (6%)
  starting transfers between devices  10 us (4%)
    all_gather x1, waiting for transfers between devices, shards(): piece = lax.all_gather(key_value, 'seq', axis=0, tiled=True)  64.8 us
    all_gather x1, blocking collectives, shards(): all_seg = lax.all_gather(segments, 'seq', axis=0, tiled=True)  46.9 us
    dot_general x16, matrix products, per_head(): jnp.dot(weight.astype(jnp.bfloat16), value_h, preferred_element_type=jnp....  32.1 us
    dot_general x16, matrix products, per_head(): score = jnp.dot(query, key_h.T, preferred_element_type=jnp.float32) * scale  31.4 us
    reduce_sum x16, other arithmetic, per_head(): new_total = total_h * factor + jnp.sum(weight, axis=1)  16 us
    transpose x1, local copies, waits for them, and re-layouts, shards(): values = jnp.moveaxis(split_piece[:, :, 1, :], 1, 0)  11.8 us
    all_to_all x1, starting transfers between devices, shards(): lax.all_to_all(key_value, 'seq', split_axis=1, concat_axis=0, tiled=True)  9.98 us
    dot_general x1, matrix products, shards(): jnp.dot(tokens, qkv_weight, preferred_element_type=jnp.float32)  6.04 us
  transfers between devices with their start and end apart: 2, of which 1 were waited for; matrix products, arithmetic and copies ran while one was open for 1% of the time, Pallas kernels for 0%

commit v1 on v0

--- a/solution.py
+++ b/solution.py
@@ -15,7 +15,10 @@
     proj = jnp.dot(tokens, qkv_weight, preferred_element_type=jnp.float32).astype(jnp.bfloat16)
     grouped = proj.reshape(tok_rows, HEADS, 3, HEAD)
     key_value = grouped[:, :, 1:, :].reshape(tok_rows, 2 * width)
-    kv_cache = lax.all_to_all(key_value, "seq", split_axis=1, concat_axis=0, tiled=True)
+    kv_cache = jnp.concatenate(
+        lax.all_to_all(jnp.stack(jnp.split(key_value, lax.axis_size("seq"), axis=1)), "seq", 0, 0),
+        axis=0,
+    )
     queries = jnp.moveaxis(grouped[:, :, 0, :], 1, 0)
     piece = lax.all_gather(key_value, "seq", axis=0, tiled=True)
     top_now = jnp.full((HEADS, tok_rows), -1e30, jnp.float32)

time: 248 us -> 252 us (1.016)
  local copies, waits for them, and re-layouts: 20.6 us -> 44.2 us
  waiting for transfers between devices: 64.8 us -> 45.2 us
    unnamed x12 -> x27, local copies, waits for them, and re-layouts: 0.03 us -> 22.1 us
    all_gather x1, waiting for transfers between devices: 64.8 us -> 45.2 us  [shards(): piece = lax.all_gather(key_value, 'seq', axis=0, tiled=True)]
  transfers between devices with their start and end apart: 2 -> 2, of which waited for: 1 -> 1; matrix products, arithmetic and copies ran while one was open for 1% -> 11% of each run, Pallas kernels for 0% -> 0%
where the time goes in v1:
time: 252 us; the launch traced here: 250 us
  matrix products  71.4 us (28%)
  blocking collectives  46.5 us (18%)
  waiting for transfers between devices  45.2 us (18%)
  local copies, waits for them, and re-layouts  44.2 us (18%)
  other arithmetic  17.7 us (7%)
  between operations  14.1 us (6%)
  starting transfers between devices  9.98 us (4%)
    all_gather x1, blocking collectives, shards(): all_seg = lax.all_gather(segments, 'seq', axis=0, tiled=True)  46.5 us
    all_gather x1, waiting for transfers between devices, shards(): piece = lax.all_gather(key_value, 'seq', axis=0, tiled=True)  45.2 us
    dot_general x16, matrix products, per_head(): jnp.dot(weight.astype(jnp.bfloat16), value_h, preferred_element_type=jnp....  32.1 us
    dot_general x16, matrix products, per_head(): score = jnp.dot(query, key_h.T, preferred_element_type=jnp.float32) * scale  31.4 us
    unnamed x27, local copies, waits for them, and re-layouts  22.1 us
    reduce_sum x16, other arithmetic, per_head(): new_total = total_h * factor + jnp.sum(weight, axis=1)  16 us
    transpose x1, local copies, waits for them, and re-layouts, shards(): values = jnp.moveaxis(split_piece[:, :, 1, :], 1, 0)  11.8 us
    all_to_all x1, starting transfers between devices, shards(): lax.all_to_all(jnp.stack(jnp.split(key_value, lax.axis_size('seq'), axis=...  9.95 us
  transfers between devices with their start and end apart: 2, of which 1 were waited for; matrix products, arithmetic and copies ran while one was open for 11% of the time, Pallas kernels for 0%

profile of v1, /device:TPU:1, one launch (start us, length us, event | category | flops | bytes accessed | tf_op | source)
XLA Modules:
  0.0 249.7 jit_solution(1339144221076870435)
XLA Ops:
  7.2 6.0 %convolution_convert_fusion = bf16[256,3072]{1,0:T(8,128)(2,1)} fusion(bf16[256,1024]{1,0:T(8,128)(2,1)} %param.9, bf16[1024,3072]{1,0:T(8,128)(2,1)} %param.11), kind=kOutput, calls=%fused_computation.24 | convolution fusion | flops 1611399168 | bytes 8388608 | tf_op jit(solution)/shard_map/dot_general | solution.py:15
  13.3 2.6 %copy.19 = bf16[256,3072]{0,1:T(8,128)(2,1)} copy(bf16[256,3072]{1,0:T(8,128)(2,1)} %convolution_convert_fusion) | data formatting | bytes 3145728 | tf_op jit(solution)/shard_map/convert_element_type | solution.py:15
  15.9 2.3 slice.17
  41.8 9.9 %all-to-all-start = ((bf16[16,256,128]{1,2,0:T(8,128)(2,1)}), bf16[16,256,128]{1,2,0:T(8,128)(2,1)S(1)}, u32[]{:S(2)}, u32[]{:S(2)}) async-start(bf16[16,256,128]{1,2,0:T(8,128)(2,1)} %fusion.27), calls=%async_computation | async-start | bytes 2097152 | tf_op jit(solution)/shard_map/all_to_all | solution.py:19
  51.8 46.5 %all-gather = s32[16,1,256]{2,1,0:T(1,128)S(1)} all-gather(s32[1,1,256]{2,1,0:T(1,128)S(1)} %bitcast.144), channel_id=1, replica_groups=mesh['seq'=16,'rep'=16] {'seq'}, dimensions={0}, use_global_device_ids=true | all-gather | bytes 17408 | tf_op jit(solution)/shard_map/all_gather | solution.py:14
  101.5 45.2 %all-gather.3.cloned.1.call-done = bf16[4096,2048]{0,1:T(8,128)(2,1)} async-done(((bf16[256,2048]{0,1:T(8,128)(2,1)}), bf16[4096,2048]{0,1:T(8,128)(2,1)}) %all-gather.3.cloned.1.call-update) | async-done | bytes 16777232 | tf_op jit(solution)/shard_map/all_gather | solution.py:23
  146.7 11.8 %slice_bitcast_fusion = (bf16[16,4096,64]{1,2,0:T(8,128)(2,1)}, bf16[16,4096,64]{1,2,0:T(8,128)(2,1)}) fusion(bf16[4096,16,2,64]{0,3,2,1:T(8,128)(2,1)} %bitcast.120), kind=kLoop, calls=%fused_computation.22 | loop fusion | bytes 33554432 | tf_op jit(solution)/shard_map/transpose | solution.py:31
  158.5 81.0 %while.13 = (s32[]{:T(128)}, f32[16,256]{1,0:T(8,128)S(1)}, f32[16,256,64]{1,2,0:T(8,128)S(1)}, bf16[16,256,64]{1,2,0:T(8,128)(2,1)}, bf16[16,4096,64]{1,2,0:T(8...) while((s32[]{:T(128)}, f32[16,256]{1,0:T(8,128)S(1)}, ...), condition=%wide.region_3.4_spmd.clone, body=%wide.region_0.3_spmd.clone.sunk | while | flops 281035520 | bytes 13797481 | solution.py:46
  161.5 2.0 fusion.58
  166.5 2.0 fusion.58
  171.6 2.0 fusion.58
  176.7 2.0 fusion.58
  181.7 2.0 fusion.58
  186.8 2.0 fusion.58
  191.8 2.0 fusion.58
  196.9 2.0 fusion.58
  202.0 2.0 fusion.58
  207.0 2.0 fusion.58
  212.1 2.0 fusion.58
  217.1 2.0 fusion.58
  222.2 2.0 fusion.58
  227.3 2.0 fusion.58
  232.3 2.0 fusion.58
  237.4 2.0 fusion.58
  (121 shorter events, 78.5 us)
Async XLA Ops:
  7.2 232.4 %copy-start = (bf16[1024,1024]{1,0:T(8,128)(2,1)S(1)}, bf16[1024,1024]{1,0:T(8,128)(2,1)}, u32[]{:S(2)}) copy-start(bf16[1024,1024]{1,0:T(8,128)(2,1)} %param.12) | copy-start | bytes 6291460
  7.2 139.5 %all-gather.3.cloned.1.call-start = ((), (), s32[]{:S(2)}) async-start(), calls=%async_computation.1 | async-start | bytes 17825792 | tf_op jit(solution)/shard_map/all_gather | solution.py:23
  15.9 35.9 %copy-start.2 = (s32[256]{0:T(256)S(1)}, s32[256]{0:T(256)}, u32[]{:S(2)}) copy-start(s32[256]{0:T(256)} %param.10) | copy-start | bytes 3076
  41.8 58.4 %all-to-all-start = ((bf16[16,256,128]{1,2,0:T(8,128)(2,1)}), bf16[16,256,128]{1,2,0:T(8,128)(2,1)S(1)}, u32[]{:S(2)}, u32[]{:S(2)}) async-start(bf16[16,256,128]{1,2,0:T(8,128)(2,1)} %fusion.27), calls=%async_computation | async-start | bytes 2097152 | tf_op jit(solution)/shard_map/all_to_all | solution.py:19
  146.7 11.8 %copy-start.1 = (f32[16,256,64]{1,2,0:T(8,128)S(1)}, f32[16,256,64]{1,2,0:T(8,128)}, u32[]{:S(2)}) copy-start(f32[16,256,64]{1,2,0:T(8,128)} %custom-call.2) | copy-start | bytes 3145732
  158.5 81.1 %copy-start.3 = (f32[1024]{0:T(1024)S(1)}, f32[1024]{0:T(1024)}, u32[]{:S(2)}) copy-start(f32[1024]{0:T(1024)} %param.13) | copy-start | bytes 12292
  239.5 2.3 copy-start.4
  239.5 2.3 copy-start.5
Sparse Core Ops, SparseCore 0:
  18.3 128.3 all-gather.2
